TPU v7x, 32 devices: a whole 2x2x4 slice. The times are simulated.
32 devices in a mesh: groups: 2 (over y), psg: 16 (over z, x, core).
Axes of the slice: x: 2, y: 2, z: 4, core: 2. Of those that a mesh axis runs over, the one named last changes fastest.
Arguments:
- tail_hidden_states: bfloat16 [256, 8192], P('groups', 'psg'), parts along dimension 0, may hold values from -6 to 6
- passage_hidden_states: bfloat16 [2048, 8192], P(('groups', 'psg')), parts along dimension 0, may hold values from -6 to 6
- lengths: int32 [4], P('groups'), parts along dimension 0, may hold values from 1 to 768, 1024 in all
- storage_order: int32 [4], P('groups'), parts along dimension 0, may hold values from 0 to 1, each once
- orders: int32 [6, 2], P('groups'), parts along dimension 0, may hold values from 0 to 1, each once within a row
- w_query: bfloat16 [8192, 4096], P('psg'), may hold values from -1 to 1
- key_weight: bfloat16 [8192, 512], P('psg'), may hold values from -0.0625 to 0.0625
- value_weight: bfloat16 [8192, 512], P('psg'), may hold values from -0.0625 to 0.0625
- w_out: bfloat16 [4096, 8192], P(None, 'psg'), may hold values from -0.09375 to 0.09375
- norm_gain: float32 [8192], P('psg'), may hold values from 0.1 to 1.9
Outputs:
- layer_out: bfloat16 [256, 8192], P('groups', 'psg'), parts along dimension 0
There are 2 independent parts, one for each index of `groups`. A program takes and returns all parts, laid end to end along the dimension named above; an argument that names none is the same for every part. Nothing has to cross between parts.
Inputs may be any that keep to these rules, and one draw needn't show every extreme that they name: `lengths`: they sum to 1024; the largest is 768. `storage_order`: A permutation of the passages. `orders`: each row is a permutation of the passages.
All inputs are finite; a program needn't handle non-finite values.
Results may differ from a plain program's by a relative error of at most 0.01065.
The roundings to bfloat16 on the way count: a program that leaves them out, or rounds other values in their place, can miss the bound.
Values may be sent and summed in bfloat16 or wider, within the bound.
No kernel may reach another device: no remote copies, remote signals or barrier semaphores. Data moves between devices by JAX's collectives and lax.ppermute only.
A program may use at most 128 MiB of HBM per device.

v0:
```python
import jax
import jax.numpy as jnp
from jax import lax
from jax.sharding import PartitionSpec as P

MODEL_WIDTH = 8192
HEAD_SIZE = 128
theta_base = 500000.0
epsilon = 1e-05


def joined(part, axis, combine):
    gathered = jax.tree.map(lambda a: lax.all_gather(a, axis), part)

    def take(source):
        return jax.tree.map(lambda a: lax.dynamic_index_in_dim(a, source, 0, False), gathered)

    return lax.fori_loop(
        1, lax.axis_size(axis), lambda source, state: combine(state, take(source)), take(0)
    )


def rotate(vectors, places):
    half = vectors.shape[-1] // 2
    freqs = theta_base ** (-jnp.arange(half, dtype=jnp.float32) * 2.0 / vectors.shape[-1])
    angles = places.astype(jnp.float32)[:, None] * freqs[None, :]
    cosine = jnp.cos(angles)[:, None, :]
    sine = jnp.sin(angles)[:, None, :]
    first = vectors[..., :half]
    second = vectors[..., half:]
    return jnp.concatenate(
        [first * cosine - second * sine, second * cosine + first * sine], axis=-1
    )


def per_device(
    tail_hidden_states,
    passage_hidden_states,
    lengths,
    storage_order,
    orders,
    w_query,
    key_weight,
    value_weight,
    w_out,
    norm_gain,
):
    shards = lax.axis_size("psg")
    device = lax.axis_index("psg")
    row_count = passage_hidden_states.shape[0]
    tail_count = tail_hidden_states.shape[0]
    kv_heads = key_weight.shape[1] // HEAD_SIZE
    query_heads = w_query.shape[1] // HEAD_SIZE
    query_group = query_heads // kv_heads
    total_keys = row_count * shards
    query_part = jnp.dot(tail_hidden_states, w_query, preferred_element_type=jnp.float32)
    key_part = jnp.dot(tail_hidden_states, key_weight, preferred_element_type=jnp.float32)
    value_part = jnp.dot(tail_hidden_states, value_weight, preferred_element_type=jnp.float32)
    query_sum, key_sum, value_sum = lax.psum((query_part, key_part, value_part), "psg")
    tail_pos = total_keys + jnp.arange(tail_count, dtype=jnp.int32)
    query_vectors = rotate(query_sum.reshape(tail_count, query_heads, HEAD_SIZE), tail_pos).astype(
        jnp.bfloat16
    )
    query_vectors = query_vectors.reshape(tail_count, kv_heads, query_group, HEAD_SIZE)
    tail_key_rows = rotate(key_sum.reshape(tail_count, kv_heads, HEAD_SIZE), tail_pos).astype(
        jnp.bfloat16
    )
    tail_value_rows = value_sum.astype(jnp.bfloat16).reshape(tail_count, kv_heads, HEAD_SIZE)

    def add_block(piece):
        return jnp.dot(passage_hidden_states, piece, preferred_element_type=jnp.float32)

    unrotated_key = add_block(lax.all_gather(key_weight, "psg", axis=0, tiled=True))
    raw_value = add_block(lax.all_gather(value_weight, "psg", axis=0, tiled=True))
    numbers = jnp.arange(lengths.shape[0], dtype=jnp.int32)
    pick = (storage_order[:, None] == numbers[None, :]).astype(jnp.int32)
    stored_lengths = jnp.sum(pick * lengths[None, :], axis=1)
    ends = jnp.cumsum(stored_lengths)
    starts = ends - stored_lengths
    row_ids = device * row_count + jnp.arange(row_count, dtype=jnp.int32)
    slots = jnp.sum((ends[None, :] <= row_ids[:, None]).astype(jnp.int32), axis=1)
    in_slot = (slots[:, None] == numbers[None, :]).astype(jnp.int32)
    offsets = row_ids - jnp.sum(in_slot * starts[None, :], axis=1)
    passage_hot = jnp.dot(in_slot, pick)
    ordered_hot = (orders[:, :, None] == numbers[None, None, :]).astype(jnp.int32)
    ordered_lengths = jnp.sum(ordered_hot * lengths[None, None, :], axis=2)
    order_starts = jnp.cumsum(ordered_lengths, axis=1) - ordered_lengths
    placed = jnp.sum(ordered_hot * order_starts[:, :, None], axis=1)
    token_positions = (
        jnp.sum(passage_hot[None, :, :] * placed[:, None, :], axis=2) + offsets[None, :]
    )
    passage_values = raw_value.astype(jnp.bfloat16).reshape(row_count, kv_heads, HEAD_SIZE)
    unrotated_key = unrotated_key.reshape(row_count, kv_heads, HEAD_SIZE)
    scale = HEAD_SIZE ** (-0.5)
    tail_scores = (
        jnp.einsum(
            "tkgd,skd->tkgs", query_vectors, tail_key_rows, preferred_element_type=jnp.float32
        )
        * scale
    )
    causal = jnp.arange(tail_count)[None, :] <= jnp.arange(tail_count)[:, None]
    tail_scores = jnp.where(causal[:, None, None, :], tail_scores, -1e30)
    tail_top = jnp.max(tail_scores, axis=-1)

    def scores_for(places):
        keys = rotate(unrotated_key, places).astype(jnp.bfloat16)
        return (
            jnp.einsum("tkgd,nkd->tkgn", query_vectors, keys, preferred_element_type=jnp.float32)
            * scale
        )

    def local_stats(places):
        scores = scores_for(places)
        peak = jnp.maximum(jnp.max(scores, axis=-1), tail_top)
        return (peak, jnp.sum(jnp.exp(scores - peak[..., None]), axis=-1))

    def combine(first, second):
        peak = jnp.maximum(first[0], second[0])
        return (peak, first[1] * jnp.exp(first[0] - peak) + second[1] * jnp.exp(second[0] - peak))

    peaks, totals = joined(lax.map(local_stats, token_positions), "psg", combine)

    def accumulate(running, inputs):
        places, peak, partial_value = inputs
        weights = jnp.exp(scores_for(places) - peak[..., None])
        tail_weights = jnp.exp(tail_scores - peak[..., None])
        denom = (partial_value + jnp.sum(tail_weights, axis=-1))[..., None]
        shared = jnp.einsum(
            "tkgn,nkd->tkgd",
            weights.astype(jnp.bfloat16),
            passage_values,
            preferred_element_type=jnp.float32,
        )
        own = jnp.einsum(
            "tkgs,skd->tkgd",
            tail_weights.astype(jnp.bfloat16),
            tail_value_rows,
            preferred_element_type=jnp.float32,
        )
        return ((running[0] + shared / denom, running[1] + own / denom), None)

    start_sums = jnp.zeros((tail_count, kv_heads, query_group, HEAD_SIZE), jnp.float32)
    (shared_sum, own_sum), unused_slot = lax.scan(
        accumulate, (start_sums, start_sums), (token_positions, peaks, totals)
    )
    agreed_output = lax.psum(shared_sum, "psg") + own_sum
    mixed = agreed_output.reshape(tail_count, -1).astype(jnp.bfloat16)
    projected = jnp.dot(mixed, w_out, preferred_element_type=jnp.float32)
    squares = lax.psum(jnp.sum(projected * projected, axis=1), "psg")
    factor = lax.rsqrt(squares / MODEL_WIDTH + epsilon)[:, None]
    return (projected * factor * norm_gain[None, :]).astype(jnp.bfloat16)


def solution(mesh):
    placed = (
        P("groups", "psg"),
        P(("groups", "psg"), None),
        P("groups"),
        P("groups"),
        P("groups", None),
        P("psg", None),
        P("psg", None),
        P("psg", None),
        P(None, "psg"),
        P("psg"),
    )
    return jax.shard_map(
        per_device, mesh=mesh, in_specs=placed, out_specs=P("groups", "psg"), check_vma=False
    )
```

profile of v0, /device:TPU:0, one launch (start us, length us, event | category | flops | bytes accessed | tf_op | source)
XLA Modules:
  0.0 503.8 jit_solution(18444703325682669474)
XLA Ops:
  6.5 1.4 convolution_bitcast_fusion.1
  8.7 3.0 convolution_bitcast_fusion
  11.7 1.7 copy.65
  16.5 66.6 %all-reduce.8 = bf16[128,512]{1,0:T(8,128)(2,1)S(1)} all-reduce(f32[128,512]{1,0:T(8,128)S(1)} %fusion.42), channel_id=1, replica_groups=mesh['groups'=2,'psg'=16] {'psg'}, use_global_device_ids=true, to_apply=%region_17.18 | all-reduce | flops 65536 | bytes 393216 | tf_op jit(solution)/shard_map/psum | solution.py:59
  84.0 32.4 %all-reduce.7.cloned.1.call-done = (f32[128,32,128]{2,1,0:T(8,128)}, f32[128,4,128]{2,0,1:T(8,128)}) async-done(((f32[128,32,128]{2,1,0:T(8,128)}, f32[128,4,128]{2,0,1:T(8,128)}), (f32[128,32,128]{2,1,0:T(8,128)}, f32[128,4,128]{2,0,1:T(8,128)})) %all-reduce.7.cloned.1.call-update) | async-done | bytes 2359312 | tf_op jit(solution)/shard_map/psum | solution.py:59
  116.5 3.0 subtract_convert_fusion.2
  121.4 1.8 fusion.41
  123.3 1.9 copy.52
  125.2 66.9 %all-gather.5.cloned.1.call-done = bf16[8192,512]{1,0:T(8,128)(2,1)} async-done(((bf16[512,512]{1,0:T(8,128)(2,1)}), bf16[8192,512]{1,0:T(8,128)(2,1)}) %all-gather.5.cloned.1.call-update) | async-done | bytes 8388624 | tf_op jit(solution)/shard_map/all_gather | solution.py:73
  192.1 4.9 convolution_bitcast_fusion.2
  197.1 70.1 %all-gather.7.cloned.1.call-done = bf16[8192,512]{1,0:T(8,128)(2,1)} async-done(((bf16[512,512]{1,0:T(8,128)(2,1)}), bf16[8192,512]{1,0:T(8,128)(2,1)}) %all-gather.7.cloned.1.call-update) | async-done | bytes 8388624 | tf_op jit(solution)/shard_map/all_gather | solution.py:74
  267.2 4.9 fusion.31
  272.8 7.1 %while.46 = (s32[]{:T(128)}, f32[3,128,4,8]{1,3,2,0:T(8,128)S(1)}, f32[3,128,4,8]{1,3,2,0:T(8,128)S(1)}, f32[64,4,128]{2,0,1:T(8,128)S(1)}, s32[3,64]{1,0:T(4,12...) while((s32[]{:T(128)}, f32[3,128,4,8]{1,3,2,0:T(8,128)S(1)}, ...), condition=%wide.region_14.15_spmd, body=%wide.region_11.14_spmd.sunk | while | flops 68419776 | bytes 3622249 | solution.py:121
  273.1 1.8 fusion.73
  275.5 1.8 fusion.73
  277.8 1.8 fusion.73
  279.9 21.2 %all-gather.1 = f32[48,128,4,8]{1,3,2,0:T(8,128)S(1)} all-gather(f32[3,128,4,8]{1,3,2,0:T(8,128)S(1)} %get-tuple-element.367), channel_id=3, replica_groups=mesh['groups'=2,'psg'=16] {'psg'}, dimensions={0}, use_global_device_ids=true | all-gather | bytes 835584 | tf_op jit(solution)/shard_map/all_gather | solution.py:13
  301.0 20.4 %all-gather = f32[48,128,4,8]{1,3,2,0:T(8,128)S(1)} all-gather(f32[3,128,4,8]{1,3,2,0:T(8,128)S(1)} %get-tuple-element.366), channel_id=2, replica_groups=mesh['groups'=2,'psg'=16] {'psg'}, dimensions={0}, use_global_device_ids=true | all-gather | bytes 835584 | tf_op jit(solution)/shard_map/all_gather | solution.py:13
  322.3 13.5 %while.47 = (s32[]{:T(128)}, f32[3,128,4,8]{1,3,2,0:T(8,128)S(1)}, f32[3,128,4,8]{1,3,2,0:T(8,128)S(1)}, f32[16,3,128,4,8]{2,4,3,1,0:T(8,128)}, f32[16,3,128,4,8...) while((s32[]{:T(128)}, f32[3,128,4,8]{1,3,2,0:T(8,128)S(1)}, f32[3,128,4,8]{1,3,2,0:T(8,128)S(1)}, ...), condition=%wide.region_16.17_spmd, body=%wide.region_15.16_spmd.sunk | while | flops 73733 | bytes 295035 | solution.py:18
  323.2 0.9 fusion.74
  324.1 0.9 fusion.74
  325.0 0.9 fusion.74
  325.9 0.9 fusion.74
  326.8 0.9 fusion.74
  327.7 0.9 fusion.74
  328.6 0.9 fusion.74
  329.5 0.9 fusion.74
  330.4 0.9 fusion.74
  331.3 0.9 fusion.74
  332.2 0.9 fusion.74
  333.1 0.9 fusion.74
  334.0 0.9 fusion.74
  334.9 0.9 fusion.74
  335.8 27.7 %while.48 = (s32[]{:T(128)}, f32[128,4,8,128]{3,0,2,1:T(8,128)}, f32[128,4,8,128]{3,0,2,1:T(8,128)}, f32[64,4,128]{2,0,1:T(8,128)S(1)}, s32[3,64]{1,0:T(4,128)S(...) while((s32[]{:T(128)}, f32[128,4,8,128]{3,0,2,1:T(8,128)}, ...), condition=%wide.region_20.21_spmd.clone, body=%wide.region_18.20_spmd.clone.sunk | while | flops 274731200 | bytes 14337436 | solution.py:143
  335.9 1.3 fusion.79
  337.5 3.7 fusion.81
  341.2 3.2 fusion.82
  344.4 1.3 fusion.79
  346.0 4.4 fusion.81
  350.4 3.5 fusion.82
  354.0 1.3 fusion.79
  355.6 4.4 fusion.81
  360.0 3.5 fusion.82
  363.5 2.9 copy.54
  366.5 1.9 copy.55
  368.4 94.1 %all-reduce.5.cloned.1.call-done = f32[128,4,8,128]{0,3,2,1:T(8,128)} async-done(((f32[128,4,8,128]{0,3,2,1:T(8,128)}), f32[128,4,8,128]{0,3,2,1:T(8,128)}) %all-reduce.5.cloned.1.call-update) | async-done | bytes 2097168 | tf_op jit(solution)/shard_map/psum | solution.py:146
  462.5 2.0 add_convert_fusion.2
  466.2 30.4 %psum.39 = f32[128]{0:T(128)S(1)} all-reduce(f32[128]{0:T(128)S(1)} %get-tuple-element.550), channel_id=1, replica_groups=mesh['groups'=2,'psg'=16] {'psg'}, use_global_device_ids=true, to_apply=%region_23.24 | all-reduce | flops 128 | bytes 1024 | tf_op jit(solution)/shard_map/psum | solution.py:149
  (109 shorter events, 13.9 us)
Async XLA Ops:
  6.5 185.6 %copy-start = (bf16[64,8192]{1,0:T(8,128)(2,1)S(1)}, bf16[64,8192]{1,0:T(8,128)(2,1)}, u32[]{:S(2)}) copy-start(bf16[64,8192]{1,0:T(8,128)(2,1)} %param.17) | copy-start | bytes 3145732
  6.5 109.9 %all-reduce.7.cloned.1.call-start = ((), (), s32[]{:S(2)}) async-start(), calls=%async_computation.3 | async-start | bytes 4718592 | tf_op jit(solution)/shard_map/psum | solution.py:59
  13.4 1.6 copy-start.10
  13.4 1.6 copy-start.11
  13.4 2.0 copy-start.8
  13.4 2.2 copy-start.3
  13.4 2.2 copy-start.6
  13.4 178.7 %all-gather.5.cloned.1.call-start = ((), (), s32[]{:S(2)}) async-start(), calls=%async_computation | async-start | bytes 8912896 | tf_op jit(solution)/shard_map/all_gather | solution.py:73
  14.2 253.0 %all-gather.7.cloned.1.call-start = ((), (), s32[]{:S(2)}) async-start(), calls=%async_computation.1 | async-start | bytes 8912896 | tf_op jit(solution)/shard_map/all_gather | solution.py:74
  14.9 447.6 %all-reduce.5.cloned.1.call-start = ((), (), s32[]{:S(2)}) async-start(), calls=%async_computation.2 | async-start | bytes 4194304 | tf_op jit(solution)/shard_map/psum | solution.py:146
  120.3 1.0 copy-start.7
  120.9 2.3 copy-start.1
  301.0 20.4 %copy-start.4 = (f32[48,128,4,8]{1,3,2,0:T(8,128)}, f32[48,128,4,8]{1,3,2,0:T(8,128)S(1)}, u32[]{:S(2)}) copy-start(f32[48,128,4,8]{1,3,2,0:T(8,128)S(1)} %all-gather.1) | copy-start | bytes 2359300
  321.5 0.9 copy-start.5
  462.5 2.8 copy-start.2
  465.3 31.2 %copy-start.9 = (f32[512]{0:T(512)S(1)}, f32[512]{0:T(512)}, u32[]{:S(2)}) copy-start(f32[512]{0:T(512)} %param.25) | copy-start | bytes 6148
Sparse Core Ops, SparseCore 0:
  13.6 102.8 all-reduce.6
  118.6 73.4 all-gather.4
  194.3 72.8 all-gather.6
  366.6 95.8 all-reduce.4
where the time goes:
time: 505 us; the launch traced here: 504 us
  waiting for transfers between devices  265 us (52%)
  blocking collectives  139 us (28%)
  matrix products  45.4 us (9%)
  other arithmetic  27.3 us (5%)
  local copies, waits for them, and re-layouts  13.5 us (3%)
  between operations  13.4 us (3%)
    psum x1, waiting for transfers between devices, per_device(): agreed_output = lax.psum(shared_sum, 'psg') + own_sum  94.1 us
    all_gather x1, waiting for transfers between devices, per_device(): lax.all_gather(value_weight, 'psg', axis=0, tiled=True)  70.1 us
    all_gather x1, waiting for transfers between devices, per_device(): lax.all_gather(key_weight, 'psg', axis=0, tiled=True)  66.9 us
    psum x1, blocking collectives, per_device(): lax.psum((query_part, key_part, value_part), 'psg')  66.6 us
    all_gather x2, blocking collectives, joined(): gathered = jax.tree.map(lambda a: lax.all_gather(a, axis), part)  41.6 us
    psum x1, waiting for transfers between devices, per_device(): lax.psum((query_part, key_part, value_part), 'psg')  32.4 us
    psum x1, blocking collectives, per_device(): squares = lax.psum(jnp.sum(projected * projected, axis=1), 'psg')  30.4 us
    add x15, other arithmetic, combine(): first[1] * jnp.exp(first[0] - peak) + second[1] * jnp.exp(second[0] - peak)  13.2 us
  transfers between devices with their start and end apart: 4, of which 4 were waited for; matrix products, arithmetic and copies ran while one was open for 3% of the time, Pallas kernels for 0%

commit v1 on v0

--- a/solution.py
+++ b/solution.py
@@ -7,6 +7,11 @@
 HEAD_SIZE = 128
 theta_base = 500000.0
 epsilon = 1e-05
+
+
+def summed_here(x, mesh_axis):
+    parts = lax.all_gather(x, mesh_axis)
+    return jnp.sum(parts, axis=0)
 
 
 def joined(part, axis, combine):
@@ -143,7 +148,7 @@
     (shared_sum, own_sum), unused_slot = lax.scan(
         accumulate, (start_sums, start_sums), (token_positions, peaks, totals)
     )
-    agreed_output = lax.psum(shared_sum, "psg") + own_sum
+    agreed_output = summed_here(shared_sum, "psg") + own_sum
     mixed = agreed_output.reshape(tail_count, -1).astype(jnp.bfloat16)
     projected = jnp.dot(mixed, w_out, preferred_element_type=jnp.float32)
     squares = lax.psum(jnp.sum(projected * projected, axis=1), "psg")

time: 505 us -> 588 us (1.16)
  waiting for transfers between devices: 265 us -> 337 us
  other arithmetic: 27.3 us -> 39 us
    all_gather x0 -> x1, waiting for transfers between devices: none -> 166 us  [summed_here(): parts = lax.all_gather(x, mesh_axis)]
    psum x1 -> x0, waiting for transfers between devices: 94.1 us -> none  [per_device(): agreed_output = lax.psum(shared_sum, 'psg') + own_sum]
    reduce_sum x0 -> x1, other arithmetic: none -> 11.8 us  [summed_here(): return jnp.sum(parts, axis=0)]
where the time goes in v1:
time: 588 us; the launch traced here: 586 us
  waiting for transfers between devices  337 us (57%)
  blocking collectives  140 us (24%)
  matrix products  46.6 us (8%)
  other arithmetic  39 us (7%)
  between operations  13.4 us (2%)
  local copies, waits for them, and re-layouts  8.51 us (1%)
    all_gather x1, waiting for transfers between devices, summed_here(): parts = lax.all_gather(x, mesh_axis)  166 us
    all_gather x1, waiting for transfers between devices, per_device(): lax.all_gather(value_weight, 'psg', axis=0, tiled=True)  70.1 us
    all_gather x1, waiting for transfers between devices, per_device(): lax.all_gather(key_weight, 'psg', axis=0, tiled=True)  66.9 us
    psum x1, blocking collectives, per_device(): lax.psum((query_part, key_part, value_part), 'psg')  66.5 us
    all_gather x2, blocking collectives, joined(): gathered = jax.tree.map(lambda a: lax.all_gather(a, axis), part)  41.2 us
    psum x1, blocking collectives, per_device(): squares = lax.psum(jnp.sum(projected * projected, axis=1), 'psg')  32.6 us
    psum x1, waiting for transfers between devices, per_device(): lax.psum((query_part, key_part, value_part), 'psg')  32.4 us
    add x15, other arithmetic, combine(): first[1] * jnp.exp(first[0] - peak) + second[1] * jnp.exp(second[0] - peak)  13.2 us
  transfers between devices with their start and end apart: 4, of which 4 were waited for; matrix products, arithmetic and copies ran while one was open for 3% of the time, Pallas kernels for 0%

profile of v1, /device:TPU:0, one launch (start us, length us, event | category | flops | bytes accessed | tf_op | source)
XLA Modules:
  0.0 586.0 jit_solution(15592702222840255161)
XLA Ops:
  6.5 1.4 convolution_bitcast_fusion.1
  8.7 3.0 convolution_bitcast_fusion
  11.7 1.7 copy.62
  16.4 66.5 %all-reduce.5 = bf16[128,512]{1,0:T(8,128)(2,1)S(1)} all-reduce(f32[128,512]{1,0:T(8,128)S(1)} %fusion.42), channel_id=1, replica_groups=mesh['groups'=2,'psg'=16] {'psg'}, use_global_device_ids=true, to_apply=%region_17.18 | all-reduce | flops 65536 | bytes 393216 | tf_op jit(solution)/shard_map/psum | solution.py:64
  84.0 32.4 %all-reduce.4.cloned.1.call-done = (f32[128,32,128]{2,1,0:T(8,128)}, f32[128,4,128]{2,0,1:T(8,128)}) async-done(((f32[128,32,128]{2,1,0:T(8,128)}, f32[128,4,128]{2,0,1:T(8,128)}), (f32[128,32,128]{2,1,0:T(8,128)}, f32[128,4,128]{2,0,1:T(8,128)})) %all-reduce.4.cloned.1.call-update) | async-done | bytes 2359312 | tf_op jit(solution)/shard_map/psum | solution.py:64
  116.4 3.0 subtract_convert_fusion.2
  121.4 1.8 fusion.41
  123.2 1.9 copy.50
  125.2 66.9 %all-gather.7.cloned.1.call-done = bf16[8192,512]{1,0:T(8,128)(2,1)} async-done(((bf16[512,512]{1,0:T(8,128)(2,1)}), bf16[8192,512]{1,0:T(8,128)(2,1)}) %all-gather.7.cloned.1.call-update) | async-done | bytes 8388624 | tf_op jit(solution)/shard_map/all_gather | solution.py:78
  192.1 4.9 convolution_bitcast_fusion.2
  197.0 70.1 %all-gather.9.cloned.1.call-done = bf16[8192,512]{1,0:T(8,128)(2,1)} async-done(((bf16[512,512]{1,0:T(8,128)(2,1)}), bf16[8192,512]{1,0:T(8,128)(2,1)}) %all-gather.9.cloned.1.call-update) | async-done | bytes 8388624 | tf_op jit(solution)/shard_map/all_gather | solution.py:79
  267.1 4.9 fusion.31
  272.7 7.1 %while.46 = (s32[]{:T(128)}, f32[3,128,4,8]{1,3,2,0:T(8,128)S(1)}, f32[3,128,4,8]{1,3,2,0:T(8,128)S(1)}, f32[64,4,128]{2,0,1:T(8,128)S(1)}, s32[3,64]{1,0:T(4,12...) while((s32[]{:T(128)}, f32[3,128,4,8]{1,3,2,0:T(8,128)S(1)}, ...), condition=%wide.region_14.15_spmd, body=%wide.region_11.14_spmd.sunk | while | flops 68419776 | bytes 3622249 | solution.py:126
  273.0 1.8 fusion.73
  275.4 1.8 fusion.73
  277.8 1.8 fusion.73
  279.8 21.3 %all-gather.1 = f32[48,128,4,8]{1,3,2,0:T(8,128)S(1)} all-gather(f32[3,128,4,8]{1,3,2,0:T(8,128)S(1)} %get-tuple-element.367), channel_id=3, replica_groups=mesh['groups'=2,'psg'=16] {'psg'}, dimensions={0}, use_global_device_ids=true | all-gather | bytes 835584 | tf_op jit(solution)/shard_map/all_gather | solution.py:18
  301.1 19.9 %all-gather = f32[48,128,4,8]{1,3,2,0:T(8,128)S(1)} all-gather(f32[3,128,4,8]{1,3,2,0:T(8,128)S(1)} %get-tuple-element.366), channel_id=2, replica_groups=mesh['groups'=2,'psg'=16] {'psg'}, dimensions={0}, use_global_device_ids=true | all-gather | bytes 835584 | tf_op jit(solution)/shard_map/all_gather | solution.py:18
  321.9 13.5 %while.47 = (s32[]{:T(128)}, f32[3,128,4,8]{1,3,2,0:T(8,128)S(1)}, f32[3,128,4,8]{1,3,2,0:T(8,128)S(1)}, f32[16,3,128,4,8]{2,4,3,1,0:T(8,128)}, f32[16,3,128,4,8...) while((s32[]{:T(128)}, f32[3,128,4,8]{1,3,2,0:T(8,128)S(1)}, f32[3,128,4,8]{1,3,2,0:T(8,128)S(1)}, ...), condition=%wide.region_16.17_spmd, body=%wide.region_15.16_spmd.sunk | while | flops 73733 | bytes 295035 | solution.py:23
  322.8 0.9 fusion.74
  323.7 0.9 fusion.74
  324.6 0.9 fusion.74
  325.5 0.9 fusion.74
  326.4 0.9 fusion.74
  327.3 0.9 fusion.74
  328.2 0.9 fusion.74
  329.1 0.9 fusion.74
  330.0 0.9 fusion.74
  330.9 0.9 fusion.74
  331.8 0.9 fusion.74
  332.7 0.9 fusion.74
  333.6 0.9 fusion.74
  334.5 0.9 fusion.74
  335.4 26.6 %while.48 = (s32[]{:T(128)}, f32[128,4,8,128]{3,0,2,1:T(8,128)}, f32[128,4,8,128]{3,0,2,1:T(8,128)}, f32[64,4,128]{2,0,1:T(8,128)S(1)}, s32[3,64]{1,0:T(4,128)S(...) while((s32[]{:T(128)}, f32[128,4,8,128]{3,0,2,1:T(8,128)}, ...), condition=%wide.region_20.21_spmd.clone, body=%wide.region_18.20_spmd.clone.sunk | while | flops 274731200 | bytes 14337436 | solution.py:148
  335.5 1.3 fusion.79
  337.1 3.2 fusion.81
  340.3 3.2 fusion.82
  343.6 1.3 fusion.79
  345.2 4.0 fusion.81
  349.3 3.5 fusion.82
  352.8 1.3 fusion.79
  354.4 4.0 fusion.81
  358.5 3.5 fusion.82
  362.0 166.5 %all-gather.11.cloned.1.call-done = f32[2048,4,8,128]{3,0,2,1:T(8,128)} async-done(((f32[128,4,8,128]{3,0,2,1:T(8,128)}), f32[2048,4,8,128]{3,0,2,1:T(8,128)}) %all-gather.11.cloned.1.call-update) | async-done | bytes 33554448 | tf_op jit(solution)/shard_map/all_gather | solution.py:13
  528.5 11.8 %reduce_sum.102 = f32[128,4,8,128]{3,0,2,1:T(8,128)S(1)} reduce(f32[16,128,4,8,128]{4,1,0,3,2:T(8,128)} %bitcast.158, f32[]{:T(128)} %constant.166.clone.1), dimensions={0}, to_apply=%region_21.22 | reduce | flops 7864320 | bytes 35651588 | tf_op jit(solution)/shard_map/reduce_sum | solution.py:14
  540.3 1.9 add_convert_fusion.2
  542.9 3.1 multiply_reduce_fusion
  546.0 32.6 %psum.31 = f32[128]{0:T(128)S(1)} all-reduce(f32[128]{0:T(128)S(1)} %get-tuple-element.550), channel_id=1, replica_groups=mesh['groups'=2,'psg'=16] {'psg'}, use_global_device_ids=true, to_apply=%region_23.24 | all-reduce | flops 128 | bytes 1024 | tf_op jit(solution)/shard_map/psum | solution.py:154
  (111 shorter events, 13.0 us)
Async XLA Ops:
  6.5 185.5 %copy-start = (bf16[64,8192]{1,0:T(8,128)(2,1)S(1)}, bf16[64,8192]{1,0:T(8,128)(2,1)}, u32[]{:S(2)}) copy-start(bf16[64,8192]{1,0:T(8,128)(2,1)} %param.17) | copy-start | bytes 3145732
  6.5 109.9 %all-reduce.4.cloned.1.call-start = ((), (), s32[]{:S(2)}) async-start(), calls=%async_computation.3 | async-start | bytes 4718592 | tf_op jit(solution)/shard_map/psum | solution.py:64
  13.3 1.6 copy-start.11
  13.3 1.6 copy-start.12
  13.3 2.0 copy-start.9
  13.3 2.2 copy-start.4
  13.3 2.2 copy-start.7
  13.4 178.7 %all-gather.7.cloned.1.call-start = ((), (), s32[]{:S(2)}) async-start(), calls=%async_computation | async-start | bytes 8912896 | tf_op jit(solution)/shard_map/all_gather | solution.py:78
  14.1 253.0 %all-gather.9.cloned.1.call-start = ((), (), s32[]{:S(2)}) async-start(), calls=%async_computation.1 | async-start | bytes 8912896 | tf_op jit(solution)/shard_map/all_gather | solution.py:79
  14.9 513.6 %all-gather.11.cloned.1.call-start = ((), (), s32[]{:S(2)}) async-start(), calls=%async_computation.2 | async-start | bytes 35651584 | tf_op jit(solution)/shard_map/all_gather | solution.py:13
  120.3 1.0 copy-start.8
  120.9 2.3 copy-start.2
  279.8 55.6 %copy-start.3 = (bf16[128,4,8,128]{3,0,2,1:T(8,128)(2,1)S(1)}, bf16[128,4,8,128]{3,0,2,1:T(8,128)(2,1)}, u32[]{:S(2)}) copy-start(bf16[128,4,8,128]{3,0,2,1:T(8,128)(2,1)} %get-tuple-element.816) | copy-start | bytes 3145732
  301.1 20.0 %copy-start.5 = (f32[48,128,4,8]{1,3,2,0:T(8,128)}, f32[48,128,4,8]{1,3,2,0:T(8,128)S(1)}, u32[]{:S(2)}) copy-start(f32[48,128,4,8]{1,3,2,0:T(8,128)S(1)} %all-gather.1) | copy-start | bytes 2359300
  321.0 0.9 copy-start.6
  542.9 36.5 %copy-start.1 = (bf16[64,8192]{1,0:T(8,128)(2,1)S(1)}, bf16[64,8192]{1,0:T(8,128)(2,1)}, u32[]{:S(2)}) copy-start(bf16[64,8192]{1,0:T(8,128)(2,1)} %param.17) | copy-start | bytes 3145732
  542.9 35.8 %copy-start.10 = (f32[512]{0:T(512)S(1)}, f32[512]{0:T(512)}, u32[]{:S(2)}) copy-start(f32[512]{0:T(512)} %param.25) | copy-start | bytes 6148
Sparse Core Ops, SparseCore 0:
  13.5 102.8 all-reduce.3
  118.6 73.4 all-gather.6
  194.2 72.8 all-gather.8
  362.1 166.3 all-gather.10
